TPU v7x, 512 devices: a whole 4x8x8 slice. The times are simulated.
512 devices in a mesh: dp: 32 (over x, y), segment: 2 (over core), mp: 8 (over z).
Axes of the slice: x: 4, y: 8, z: 8, core: 2. Of those that a mesh axis runs over, the one named last changes fastest.
Arguments:
- frames: bfloat16 [2, 8192, 1280], P(None, ('dp', 'mp')), may hold values from -8 to 8
- dec_states: bfloat16 [2, 2048, 1280], P(None, 'dp'), may hold values from -8 to 8
- out_grad: bfloat16 [2, 2048, 1280], P(None, 'dp'), may hold values from -3 to 3
- frame_lengths: int32 [2, 32, 4], P(None, 'dp'), may hold values from 1 to 128, 256 in all within a row
- token_lengths: int32 [2, 32, 4], P(None, 'dp'), may hold values from 1 to 32, 64 in all within a row
- weights: bfloat16 [2, 4, 1024, 1280], P('segment', None, 'mp'), may hold values from -1 to 1
- norm_gains: float32 [3, 1280], replicated, may hold values from 0.25 to 1.75
- norm_biases: float32 [3, 1280], replicated, may hold values from -2 to 2
Outputs:
- gradient: float32 [2, 3, 1024, 1280], P('segment', None, 'mp')
Inputs may be any that keep to these rules, and one draw needn't show every extreme that they name: `frame_lengths`: the 4 utterance lengths of each micro-batch and group sum to 256. `token_lengths`: the 4 token counts of each micro-batch and group sum to 64.
All inputs are finite; a program needn't handle non-finite values.
Results may differ from a plain program's by a relative error of at most 0.04.
Values may be sent and summed in bfloat16 or wider, within the bound.
No kernel may reach another device: no remote copies, remote signals or barrier semaphores. Data moves between devices by JAX's collectives and lax.ppermute only.
A program may use at most 64 MiB of HBM per device.

v0:
```python
import math
import jax
import jax.numpy as jnp
from jax import lax
from jax.sharding import PartitionSpec as P

HS = 64
EPSILON = 1e-05
ROWS_DIMS = (((0,), (0,)), ((), ()))
FEAT_DIMS = (((1,), (1,)), ((), ()))


def layer_norm(values, norm_gain, offset):
    center = values - jnp.mean(values, axis=-1, keepdims=True)
    variance = jnp.mean(center * center, axis=-1, keepdims=True)
    return center * lax.rsqrt(variance + EPSILON) * norm_gain + offset


def norm_backward(grad_out, values, norm_gain):
    center = values - jnp.mean(values, axis=-1, keepdims=True)
    variance = jnp.mean(center * center, axis=-1, keepdims=True)
    inverse = lax.rsqrt(variance + EPSILON)
    normed = center * inverse
    scaled = grad_out * norm_gain
    return inverse * (
        scaled
        - jnp.mean(scaled, axis=-1, keepdims=True)
        - normed * jnp.mean(scaled * normed, axis=-1, keepdims=True)
    )


def utterance_ids(lengths, row_count):
    bounds = jnp.cumsum(lengths, dtype=jnp.int32)
    places = jnp.arange(row_count, dtype=jnp.int32)
    return jnp.sum((places[:, None] >= bounds[None, :]).astype(jnp.int32), axis=1)


def project(row_block, matrix):
    return lax.dot_general(row_block, matrix, FEAT_DIMS, preferred_element_type=jnp.float32).astype(
        jnp.bfloat16
    )


def outer_rows(left_rows, right_rows):
    return lax.dot_general(left_rows, right_rows, ROWS_DIMS, preferred_element_type=jnp.float32)


def split_heads(row_block):
    return row_block.reshape(row_block.shape[0], -1, HS)


def attend(queries, key_rows, value_rows, allowed):
    scaling = 1.0 / math.sqrt(HS)
    scores = (
        jnp.einsum(
            "qhd,khd->hqk",
            split_heads(queries),
            split_heads(key_rows),
            preferred_element_type=jnp.float32,
        )
        * scaling
    )
    scores = jnp.where(allowed[None], scores, -1e30)
    highest = jnp.max(scores, axis=-1, keepdims=True)
    raised = jnp.exp(scores - highest)
    attn_probs = raised / jnp.sum(raised, axis=-1, keepdims=True)
    context = jnp.einsum(
        "hqk,khd->qhd",
        attn_probs.astype(jnp.bfloat16),
        split_heads(value_rows),
        preferred_element_type=jnp.float32,
    )
    return (context.reshape(queries.shape[0], -1).astype(jnp.bfloat16), attn_probs)


def attend_backward(queries, key_rows, value_rows, attn_probs, grad_context):
    scaling = 1.0 / math.sqrt(HS)
    grad_heads = split_heads(grad_context)
    grad_probs = jnp.einsum(
        "qhd,khd->hqk", grad_heads, split_heads(value_rows), preferred_element_type=jnp.float32
    )
    grad_scores = (
        attn_probs * (grad_probs - jnp.sum(grad_probs * attn_probs, axis=-1, keepdims=True))
    ).astype(jnp.bfloat16)
    key_grad = (
        jnp.einsum(
            "hqk,qhd->khd", grad_scores, split_heads(queries), preferred_element_type=jnp.float32
        )
        * scaling
    )
    key_grad = key_grad.reshape(key_rows.shape[0], -1).astype(jnp.bfloat16)
    value_grad = jnp.einsum(
        "hqk,qhd->khd",
        attn_probs.astype(jnp.bfloat16),
        grad_heads,
        preferred_element_type=jnp.float32,
    )
    value_grad = value_grad.reshape(key_rows.shape[0], -1).astype(jnp.bfloat16)
    return (key_grad, value_grad)


def spread(block, axis):
    size = lax.axis_size(axis)
    return lax.all_to_all(jnp.broadcast_to(block[None], (size,) + block.shape), axis, 0, 0)


def share_sum(blocks, axis):
    return jnp.sum(lax.all_to_all(blocks, axis, 0, 0).astype(jnp.float32), axis=0)


def swap(block):
    return lax.ppermute(block, "segment", [(0, 1), (1, 0)])


def to_chunks(block, parts):
    high, wide = (block.shape[0] // 8, block.shape[1] // 128)
    tiles = block.reshape(high, 8, wide, 128).transpose(0, 2, 1, 3).reshape(-1, 8, 128)
    each = -(-tiles.shape[0] // parts)
    tiles = jnp.pad(tiles, ((0, each * parts - tiles.shape[0]), (0, 0), (0, 0)))
    return tiles.reshape(parts, each, 8, 128)


def from_chunks(chunks, rows, cols):
    high, wide = (rows // 8, cols // 128)
    tiles = chunks.reshape(-1, 8, 128)[: high * wide]
    return tiles.reshape(high, wide, 8, 128).transpose(0, 2, 1, 3).reshape(rows, cols)


def shards(
    frames, dec_states, out_grad, frame_lengths, token_lengths, weights, norm_gains, norm_biases
):
    core = lax.axis_index("segment")
    first = core == 0
    own = weights[0]
    shard_rows, features = frames.shape[1:]
    mp = lax.axis_size("mp")
    dp = lax.axis_size("dp")
    head_cols = own.shape[1]
    rows = shard_rows * mp
    half = features // 2

    def mine(array):
        return lax.dynamic_index_in_dim(array, core, 0, keepdims=False)

    inputs = mine(frames)
    tokens = mine(dec_states)
    upstream = mine(out_grad)
    frame_ids = utterance_ids(mine(frame_lengths)[0], rows)
    token_ids = utterance_ids(mine(token_lengths)[0], tokens.shape[0])
    out_sent = lax.ppermute(own[3, :, half:], "segment", [(0, 1)])
    out_part = jnp.where(first, own[3, :, :half], out_sent)
    out_part = lax.all_gather(out_part, "mp", axis=0, tiled=True)
    out_rest = swap(out_part)
    enc_full = spread(inputs, "mp").reshape(rows, features)
    other = swap(own)
    enc = jnp.where(first, own, other)
    dec = jnp.where(first, other, own)
    normed = layer_norm(enc_full.astype(jnp.float32), norm_gains[0], norm_biases[0]).astype(
        jnp.bfloat16
    )
    queries = project(normed, enc[0])
    key_rows = project(normed, enc[1])
    value_rows = project(normed, enc[2])
    context, probs = attend(queries, key_rows, value_rows, frame_ids[:, None] == frame_ids[None, :])
    context_full = spread(context, "mp").transpose(1, 0, 2).reshape(rows, mp * head_cols)
    out_mine = jnp.dot(context_full, out_part, preferred_element_type=jnp.float32)
    out_other = jnp.dot(context_full, out_rest, preferred_element_type=jnp.float32)
    summed = jnp.concatenate(
        [jnp.where(first, out_mine, out_other), jnp.where(first, out_other, out_mine)], axis=1
    )
    states_full = (enc_full.astype(jnp.float32) + summed).astype(jnp.bfloat16)
    states = lax.dynamic_slice_in_dim(states_full, lax.axis_index("mp") * shard_rows, shard_rows, 0)
    state_normed = layer_norm(
        states_full.astype(jnp.float32), norm_gains[2], norm_biases[2]
    ).astype(jnp.bfloat16)
    token_normed = layer_norm(tokens.astype(jnp.float32), norm_gains[1], norm_biases[1]).astype(
        jnp.bfloat16
    )
    dec_queries = project(token_normed, dec[0])
    dec_keys = project(state_normed, dec[1])
    dec_values = project(state_normed, dec[2])
    dec_context, dec_probs = attend(
        dec_queries, dec_keys, dec_values, token_ids[:, None] == frame_ids[None, :]
    )
    grad_context = project(upstream, dec[3])
    dec_key_grad, dec_value_grad = attend_backward(
        dec_queries, dec_keys, dec_values, dec_probs, grad_context
    )
    partial = (
        jnp.dot(dec_key_grad, dec[1], preferred_element_type=jnp.float32)
        + jnp.dot(dec_value_grad, dec[2], preferred_element_type=jnp.float32)
    ).astype(jnp.bfloat16)

    def combine(term):
        left, right = (term[:, :half], term[:, half:])
        sent = swap(jnp.where(first, right, left).astype(jnp.bfloat16))
        return (jnp.where(first, left, right) + sent.astype(jnp.float32)).astype(jnp.bfloat16)

    def reduce_groups(term):
        total = share_sum(to_chunks(term, dp), "dp").astype(jnp.bfloat16)
        return from_chunks(spread(total, "dp"), 3 * head_cols, half)

    dec_term = jnp.concatenate(
        [
            outer_rows(dec_key_grad, state_normed),
            outer_rows(dec_value_grad, state_normed),
            outer_rows(dec_context, upstream),
        ]
    )
    pieces = lax.all_to_all(partial.reshape(mp, shard_rows, features), "mp", 0, 0)
    pieces, dec_part = lax.optimization_barrier((pieces, combine(dec_term)))
    dec_total = lax.psum(dec_part, "dp")
    summed = jnp.sum(pieces.astype(jnp.float32), axis=0)
    grads = norm_backward(summed, states.astype(jnp.float32), norm_gains[2]).astype(jnp.bfloat16)
    grads_full = spread(grads, "mp").reshape(rows, features)
    att_grad = project(grads_full, enc[3])
    enc_key_grad, enc_value_grad = attend_backward(queries, key_rows, value_rows, probs, att_grad)
    enc_term = jnp.concatenate(
        [
            outer_rows(enc_key_grad, normed),
            outer_rows(enc_value_grad, normed),
            outer_rows(context, grads_full),
        ]
    )
    enc_total = reduce_groups(combine(enc_term))
    kept = jnp.where(first, enc_total, dec_total)
    got = swap(jnp.where(first, dec_total, enc_total))
    gradient = jnp.concatenate(
        [jnp.where(first, kept, got), jnp.where(first, got, kept)], axis=1
    ).astype(jnp.float32)
    return gradient.reshape(1, 3, head_cols, features)


def solution(mesh):
    placed = (
        P(None, ("dp", "mp"), None),
        P(None, "dp", None),
        P(None, "dp", None),
        P(None, "dp", None),
        P(None, "dp", None),
        P("segment", None, "mp", None),
        P(),
        P(),
    )
    return jax.shard_map(
        shards,
        mesh=mesh,
        in_specs=placed,
        out_specs=P("segment", None, "mp", None),
        check_vma=False,
    )
```

profile of v0, /device:TPU:1, one launch (start us, length us, event | category | flops | bytes accessed | tf_op | source)
XLA Modules:
  0.0 379.2 jit_solution(9192799755561751875)
XLA Ops:
  8.5 10.9 %all-to-all-start = ((bf16[8,32,1280]{2,1,0:T(8,128)(2,1)}), bf16[8,32,1280]{2,1,0:T(8,128)(2,1)S(1)}, u32[]{:S(2)}, u32[]{:S(2)}) async-start(bf16[8,32,1280]{2,1,0:T(8,128)(2,1)} %broadcast_in_dim.31), calls=%async_computation | async-start | bytes 1310720 | tf_op jit(solution)/shard_map/all_to_all | solution.py:104
  19.4 2.9 collective-permute-start
  27.3 12.8 %all-to-all-done = bf16[8,32,1280]{2,1,0:T(8,128)(2,1)S(1)} async-done(((bf16[8,32,1280]{2,1,0:T(8,128)(2,1)}), bf16[8,32,1280]{2,1,0:T(8,128)(2,1)S(1)}, u32[]{:S(2)}, u32[]{:S(2)}) %all-to-all-start) | async-done | bytes 655392 | tf_op jit(solution)/shard_map/all_to_all | solution.py:104
  41.4 1.5 broadcast_select_fusion.1
  44.4 23.2 %all-gather.2.cloned.1.call-done = bf16[1024,640]{1,0:T(8,128)(2,1)} async-done(((bf16[128,640]{1,0:T(8,128)(2,1)}), bf16[1024,640]{1,0:T(8,128)(2,1)}) %all-gather.2.cloned.1.call-update) | async-done | bytes 1310736 | tf_op jit(solution)/shard_map/all_gather | solution.py:152
  67.6 7.2 %collective-permute-start.2 = (bf16[1024,640]{1,0:T(8,128)(2,1)}, bf16[1024,640]{1,0:T(8,128)(2,1)}, u32[]{:S(2)}, u32[]{:S(2)}) collective-permute-start(bf16[1024,640]{1,0:T(8,128)(2,1)} %all-gather.2.cloned.1.call-done), channel_id=1, source_target_pairs={{0,8},{8,0},{1,9},{9,1},{2,10},{10,2},{3,11},{11,3},{4,12},{12,4},... | collective-permute-start | bytes 3932168 | tf_op jit(solution)/shard_map/ppermute | solution.py:112
  77.4 3.9 %all-to-all-start.1 = ((bf16[8,256,128]{1,2,0:T(8,128)(2,1)}), bf16[8,256,128]{1,2,0:T(8,128)(2,1)S(1)}, u32[]{:S(2)}, u32[]{:S(2)}) async-start(bf16[8,256,128]{1,2,0:T(8,128)(2,1)} %broadcast_in_dim.34), calls=%async_computation.1 | async-start | bytes 1048576 | tf_op jit(solution)/shard_map/all_to_all | solution.py:104
  83.4 1.4 copy.34
  85.7 1.4 copy.35
  87.1 12.2 %all-to-all-done.1 = bf16[8,256,128]{1,2,0:T(8,128)(2,1)S(1)} async-done(((bf16[8,256,128]{1,2,0:T(8,128)(2,1)}), bf16[8,256,128]{1,2,0:T(8,128)(2,1)S(1)}, u32[]{:S(2)}, u32[]{:S(2)}) %all-to-all-start.1) | async-done | bytes 524320 | tf_op jit(solution)/shard_map/all_to_all | solution.py:104
  99.3 1.9 fusion.72
  101.2 1.9 broadcast_select_fusion.7
  107.3 2.4 fusion.25
  111.0 1.3 fusion.17
  114.6 2.2 fusion.2
  116.8 3.5 all-to-all-start.2
  120.3 1.6 pad_maximum_fusion
  122.0 2.4 collective-permute-start.3
  126.9 14.1 %all-to-all-done.2 = bf16[8,32,1280]{2,1,0:T(8,128)(2,1)S(1)} async-done(((bf16[8,32,1280]{2,1,0:T(8,128)(2,1)}), bf16[8,32,1280]{2,1,0:T(8,128)(2,1)S(1)}, u32[]{:S(2)}, u32[]{:S(2)}) %all-to-all-start.2) | async-done | bytes 655392 | tf_op jit(solution)/shard_map/all_to_all | solution.py:210
  141.5 22.3 %all_to_all.30 = bf16[8,32,1280]{2,1,0:T(8,128)(2,1)S(1)} all-to-all(bf16[8,32,1280]{2,1,0:T(8,128)(2,1)S(1)} %broadcast_in_dim.37), channel_id=1, replica_groups=mesh['dp'=32,'segment'=2,'mp'=8] {'mp'}, dimensions={0} | all-to-all | bytes 1310720 | tf_op jit(solution)/shard_map/all_to_all | solution.py:104
  163.8 1.4 convolution_convert_fusion
  165.5 1.5 convolution_convert_fusion.7
  167.3 1.4 fusion.16
  169.5 3.2 collective-permute-start.4
  172.7 1.5 collective-permute-done.4
  174.4 23.2 %all_to_all.31 = bf16[32,8,8,128]{3,2,1,0:T(8,128)(2,1)S(1)} all-to-all(bf16[32,8,8,128]{3,2,1,0:T(8,128)(2,1)S(1)} %bitcast.176), channel_id=1, replica_groups=mesh['dp'=32,'segment'=2,'mp'=8] {'dp'}, dimensions={0} | all-to-all | bytes 1048576 | tf_op jit(solution)/shard_map/all_to_all | solution.py:108
  198.6 8.1 %all-to-all-start.5 = ((bf16[32,8,8,128]{3,2,1,0:T(8,128)(2,1)}), bf16[32,8,8,128]{3,2,1,0:T(8,128)(2,1)S(1)}, u32[]{:S(2)}, u32[]{:S(2)}) async-start(bf16[32,8,8,128]{3,2,1,0:T(8,128)(2,1)} %broadcast_in_dim.42), calls=%async_computation.5 | async-start | bytes 1048576 | tf_op jit(solution)/shard_map/all_to_all | solution.py:104
  207.5 13.3 %all-to-all-done.5 = bf16[32,8,8,128]{3,2,1,0:T(8,128)(2,1)S(1)} async-done(((bf16[32,8,8,128]{3,2,1,0:T(8,128)(2,1)}), bf16[32,8,8,128]{3,2,1,0:T(8,128)(2,1)S(1)}, u32[]{:S(2)}, u32[]{:S(2)}) %all-to-all-start.5) | async-done | bytes 524320 | tf_op jit(solution)/shard_map/all_to_all | solution.py:104
  220.8 140.2 %all-reduce.3.cloned.1.call-done = bf16[384,640]{1,0:T(8,128)(2,1)} async-done(((bf16[384,640]{1,0:T(8,128)(2,1)}), bf16[384,640]{1,0:T(8,128)(2,1)}) %all-reduce.3.cloned.1.call-update) | async-done | bytes 491536 | tf_op jit(solution)/shard_map/psum | solution.py:212
  361.1 8.2 %collective-permute-start.5 = (bf16[384,640]{1,0:T(8,128)(2,1)S(1)}, bf16[384,640]{1,0:T(8,128)(2,1)S(1)}, u32[]{:S(2)}, u32[]{:S(2)}) collective-permute-start(bf16[384,640]{1,0:T(8,128)(2,1)S(1)} %broadcast_select_fusion.4), channel_id=1, source_target_pairs={{0,8},{8,0},{1,9},{9,1},{2,10},{10,2},{3,11},{11,3},{4,12},{12,4},... | collective-permute-start | bytes 1474568 | tf_op jit(solution)/shard_map/ppermute | solution.py:112
  369.3 1.5 collective-permute-done.5
  370.9 1.4 maximum_convert_fusion
  (142 shorter events, 29.2 us)
Async XLA Ops:
  6.5 78.3 %copy-start = (bf16[2,64,1280]{2,1,0:T(8,128)(2,1)S(1)}, bf16[2,64,1280]{2,1,0:T(8,128)(2,1)}, u32[]{:S(2)}) copy-start(bf16[2,64,1280]{2,1,0:T(8,128)(2,1)} %param.10) | copy-start | bytes 983044
  6.5 12.9 %copy-start.4 = (bf16[1,4,128,1280]{3,2,1,0:T(8,128)(2,1)S(1)}, bf16[1,4,128,1280]{3,2,1,0:T(8,128)(2,1)}, u32[]{:S(2)}) copy-start(bf16[1,4,128,1280]{3,2,1,0:T(8,128)(2,1)} %param.13) | copy-start | bytes 3932164
  6.5 17.1 %copy-start.20 = (s32[2,1,4]{2,1,0:T(1,128)S(1)}, s32[2,1,4]{2,1,0:T(1,128)}, u32[]{:S(2)}) copy-start(s32[2,1,4]{2,1,0:T(1,128)} %param.11) | copy-start | bytes 100
  6.5 17.1 %copy-start.21 = (s32[2,1,4]{2,1,0:T(1,128)S(1)}, s32[2,1,4]{2,1,0:T(1,128)}, u32[]{:S(2)}) copy-start(s32[2,1,4]{2,1,0:T(1,128)} %param.12) | copy-start | bytes 100
  6.5 17.4 %copy-start.8 = (bf16[2,64,1280]{2,1,0:T(8,128)(2,1)S(1)}, bf16[2,64,1280]{2,1,0:T(8,128)(2,1)}, u32[]{:S(2)}) copy-start(bf16[2,64,1280]{2,1,0:T(8,128)(2,1)} %param.9) | copy-start | bytes 983044
  7.6 18.3 %copy-start.14 = (f32[3,1280]{1,0:T(4,128)S(1)}, f32[3,1280]{1,0:T(4,128)}, u32[]{:S(2)}) copy-start(f32[3,1280]{1,0:T(4,128)} %param.15) | copy-start | bytes 46084
  7.6 18.3 %copy-start.15 = (f32[3,1280]{1,0:T(4,128)S(1)}, f32[3,1280]{1,0:T(4,128)}, u32[]{:S(2)}) copy-start(f32[3,1280]{1,0:T(4,128)} %param.14) | copy-start | bytes 46084
  8.5 31.6 %all-to-all-start = ((bf16[8,32,1280]{2,1,0:T(8,128)(2,1)}), bf16[8,32,1280]{2,1,0:T(8,128)(2,1)S(1)}, u32[]{:S(2)}, u32[]{:S(2)}) async-start(bf16[8,32,1280]{2,1,0:T(8,128)(2,1)} %broadcast_in_dim.31), calls=%async_computation | async-start | bytes 1310720 | tf_op jit(solution)/shard_map/all_to_all | solution.py:104
  19.3 48.2 %all-gather.2.cloned.1.call-start = ((), (), s32[]{:S(2)}) async-start(), calls=%async_computation.6 | async-start | bytes 1474560 | tf_op jit(solution)/shard_map/all_gather | solution.py:152
  19.4 21.6 %collective-permute-start = (bf16[4,128,1280]{2,1,0:T(8,128)(2,1)S(1)}, bf16[4,128,1280]{2,1,0:T(8,128)(2,1)}, u32[]{:S(2)}, u32[]{:S(2)}) collective-permute-start(bf16[4,128,1280]{2,1,0:T(8,128)(2,1)S(1)} %bitcast.177), channel_id=1, source_target_pairs={{0,8},{8,0},{1,9},{9,1},{2,10},{10,2},{3,11},{11,3},{4,12},{12,4},... | collective-permute-start | bytes 3932168 | tf_op jit(solution)/shard_map/ppermute | solution.py:112
  22.3 4.3 %collective-permute-start.1 = (bf16[128,640]{1,0:T(8,128)(2,1)S(1)}, bf16[128,640]{1,0:T(8,128)(2,1)S(1)}, u32[]{:S(2)}, u32[]{:S(2)}) collective-permute-start(bf16[128,640]{1,0:T(8,128)(2,1)S(1)} %slice_bitcast_fusion.18), channel_id=1, source_target_pairs={{0,8},{1,9},{2,10},{3,11},{4,12},{5,13},{6,14},{7,15},{16,24},{17,... | collective-permute-start | bytes 491528 | tf_op jit(solution)/shard_map/ppermute | solution.py:150
  24.0 1.9 copy-start.18
  25.3 50.7 %copy-start.10 = (pred[256,256]{0,1:T(8,128)(4,1)}, pred[256,256]{0,1:T(8,128)(4,1)S(1)}, u32[]{:S(2)}) copy-start(pred[256,256]{0,1:T(8,128)(4,1)S(1)} %broadcast_compare_fusion) | copy-start | bytes 196612
  42.9 41.9 %copy-start.2 = (bf16[4,128,1280]{2,1,0:T(8,128)(2,1)}, bf16[4,128,1280]{2,1,0:T(8,128)(2,1)S(1)}, u32[]{:S(2)}) copy-start(bf16[4,128,1280]{2,1,0:T(8,128)(2,1)S(1)} %get-tuple-element.22) | copy-start | bytes 3932164
  43.3 32.7 %copy-start.22 = (bf16[256,128]{0,1:T(8,128)(2,1)}, bf16[256,128]{0,1:T(8,128)(2,1)S(1)}, u32[]{:S(2)}) copy-start(bf16[256,128]{0,1:T(8,128)(2,1)S(1)} %convolution_convert_fusion.5) | copy-start | bytes 196612
  44.0 32.5 %copy-start.24 = (bf16[256,128]{0,1:T(8,128)(2,1)}, bf16[256,128]{0,1:T(8,128)(2,1)S(1)}, u32[]{:S(2)}) copy-start(bf16[256,128]{0,1:T(8,128)(2,1)S(1)} %convolution_convert_fusion.6) | copy-start | bytes 196612
  44.3 32.2 %copy-start.26 = (bf16[256,128]{0,1:T(8,128)(2,1)}, bf16[256,128]{0,1:T(8,128)(2,1)S(1)}, u32[]{:S(2)}) copy-start(bf16[256,128]{0,1:T(8,128)(2,1)S(1)} %convolution_convert_fusion.4) | copy-start | bytes 196612
  67.6 31.7 %collective-permute-start.2 = (bf16[1024,640]{1,0:T(8,128)(2,1)}, bf16[1024,640]{1,0:T(8,128)(2,1)}, u32[]{:S(2)}, u32[]{:S(2)}) collective-permute-start(bf16[1024,640]{1,0:T(8,128)(2,1)} %all-gather.2.cloned.1.call-done), channel_id=1, source_target_pairs={{0,8},{8,0},{1,9},{9,1},{2,10},{10,2},{3,11},{11,3},{4,12},{12,4},... | collective-permute-start | bytes 3932168 | tf_op jit(solution)/shard_map/ppermute | solution.py:112
  77.4 21.9 %all-to-all-start.1 = ((bf16[8,256,128]{1,2,0:T(8,128)(2,1)}), bf16[8,256,128]{1,2,0:T(8,128)(2,1)S(1)}, u32[]{:S(2)}, u32[]{:S(2)}) async-start(bf16[8,256,128]{1,2,0:T(8,128)(2,1)} %broadcast_in_dim.34), calls=%async_computation.1 | async-start | bytes 1048576 | tf_op jit(solution)/shard_map/all_to_all | solution.py:104
  104.0 1.7 copy-start.12
  112.4 2.2 copy-start.1
  116.8 24.2 %all-to-all-start.2 = ((bf16[8,32,1280]{2,1,0:T(8,128)(2,1)}), bf16[8,32,1280]{2,1,0:T(8,128)(2,1)S(1)}, u32[]{:S(2)}, u32[]{:S(2)}) async-start(bf16[8,32,1280]{2,1,0:T(8,128)(2,1)} %bitcast.37), calls=%async_computation.2 | async-start | bytes 1310720 | tf_op jit(solution)/shard_map/all_to_all | solution.py:210
  122.0 3.9 %collective-permute-start.3 = (bf16[384,640]{1,0:T(8,128)(2,1)S(1)}, bf16[384,640]{1,0:T(8,128)(2,1)S(1)}, u32[]{:S(2)}, u32[]{:S(2)}) collective-permute-start(bf16[384,640]{1,0:T(8,128)(2,1)S(1)} %select_convert_fusion.1), channel_id=1, source_target_pairs={{0,8},{8,0},{1,9},{9,1},{2,10},{10,2},{3,11},{11,3},{4,12},{12,4},... | collective-permute-start | bytes 1474568 | tf_op jit(solution)/shard_map/ppermute | solution.py:112
  163.8 1.7 copy-start.23
  163.8 1.7 copy-start.25
  163.8 1.7 copy-start.31
  165.4 1.5 copy-start.27
  169.5 4.7 %collective-permute-start.4 = (bf16[384,640]{1,0:T(8,128)(2,1)S(1)}, bf16[384,640]{1,0:T(8,128)(2,1)S(1)}, u32[]{:S(2)}, u32[]{:S(2)}) collective-permute-start(bf16[384,640]{1,0:T(8,128)(2,1)S(1)} %select_convert_fusion), channel_id=1, source_target_pairs={{0,8},{8,0},{1,9},{9,1},{2,10},{10,2},{3,11},{11,3},{4,12},{12,4},... | collective-permute-start | bytes 1474568 | tf_op jit(solution)/shard_map/ppermute | solution.py:112
  198.6 22.2 %all-to-all-start.5 = ((bf16[32,8,8,128]{3,2,1,0:T(8,128)(2,1)}), bf16[32,8,8,128]{3,2,1,0:T(8,128)(2,1)S(1)}, u32[]{:S(2)}, u32[]{:S(2)}) async-start(bf16[32,8,8,128]{3,2,1,0:T(8,128)(2,1)} %broadcast_in_dim.42), calls=%async_computation.5 | async-start | bytes 1048576 | tf_op jit(solution)/shard_map/all_to_all | solution.py:104
  206.7 154.3 %all-reduce.3.cloned.1.call-start = ((), (), s32[]{:S(2)}) async-start(), calls=%async_computation.7 | async-start | bytes 983040 | tf_op jit(solution)/shard_map/psum | solution.py:212
  361.0 9.8 %copy-start.6 = (bf16[384,640]{1,0:T(8,128)(2,1)S(1)}, bf16[384,640]{1,0:T(8,128)(2,1)}, u32[]{:S(2)}) copy-start(bf16[384,640]{1,0:T(8,128)(2,1)} %all-reduce.3.cloned.1.call-done) | copy-start | bytes 1474564
  361.1 9.7 %collective-permute-start.5 = (bf16[384,640]{1,0:T(8,128)(2,1)S(1)}, bf16[384,640]{1,0:T(8,128)(2,1)S(1)}, u32[]{:S(2)}, u32[]{:S(2)}) collective-permute-start(bf16[384,640]{1,0:T(8,128)(2,1)S(1)} %broadcast_select_fusion.4), channel_id=1, source_target_pairs={{0,8},{8,0},{1,9},{9,1},{2,10},{10,2},{3,11},{11,3},{4,12},{12,4},... | collective-permute-start | bytes 1474568 | tf_op jit(solution)/shard_map/ppermute | solution.py:112
  (12 other events, 15.6 us)
Sparse Core Ops, SparseCore 0:
  27.4 40.0 all-gather.1
  210.9 150.0 all-reduce.2
where the time goes:
time: 380 us; the launch traced here: 379 us
  waiting for transfers between devices  220 us (58%)
  starting transfers between devices  51.7 us (14%)
  blocking collectives  45.5 us (12%)
  matrix products  25.7 us (7%)
  between operations  14 us (4%)
  other arithmetic  13.8 us (4%)
  local copies, waits for them, and re-layouts  8.81 us (2%)
    psum x1, waiting for transfers between devices, shards(): dec_total = lax.psum(dec_part, 'dp')  140 us
    all_to_all x3, waiting for transfers between devices, spread(): lax.all_to_all(jnp.broadcast_to(block[None], (size,) + block.shape), axis...  38.3 us
    ppermute x5, starting transfers between devices, swap(): return lax.ppermute(block, 'segment', [(0, 1), (1, 0)])  23.9 us
    all_to_all x1, blocking collectives, share_sum(): lax.all_to_all(blocks, axis, 0, 0).astype(jnp.float32)  23.2 us
    all_gather x1, waiting for transfers between devices, shards(): out_part = lax.all_gather(out_part, 'mp', axis=0, tiled=True)  23.2 us
    all_to_all x3, starting transfers between devices, spread(): lax.all_to_all(jnp.broadcast_to(block[None], (size,) + block.shape), axis...  22.8 us
    all_to_all x1, blocking collectives, spread(): lax.all_to_all(jnp.broadcast_to(block[None], (size,) + block.shape), axis...  22.3 us
    all_to_all x1, waiting for transfers between devices, shards(): lax.all_to_all(partial.reshape(mp, shard_rows, features), 'mp', 0, 0)  14.1 us
  transfers between devices with their start and end apart: 12, of which 9 were waited for; matrix products, arithmetic and copies ran while one was open for 5% of the time, Pallas kernels for 0%

commit v1 on v0

--- a/solution.py
+++ b/solution.py
@@ -209,7 +209,11 @@
     )
     pieces = lax.all_to_all(partial.reshape(mp, shard_rows, features), "mp", 0, 0)
     pieces, dec_part = lax.optimization_barrier((pieces, combine(dec_term)))
-    dec_total = lax.psum(dec_part, "dp")
+    dec_total = dec_part
+    for hop in (1, 2, 4, 8, 16):
+        dec_total = dec_total + lax.ppermute(
+            dec_total, "dp", [(dev, dev ^ hop) for dev in range(32)]
+        )
     summed = jnp.sum(pieces.astype(jnp.float32), axis=0)
     grads = norm_backward(summed, states.astype(jnp.float32), norm_gains[2]).astype(jnp.bfloat16)
     grads_full = spread(grads, "mp").reshape(rows, features)

time: 380 us -> 298 us (0.78)
  waiting for transfers between devices: 220 us -> 135 us
  blocking collectives: 45.5 us -> 22.3 us
  starting transfers between devices: 51.7 us -> 74.7 us
    psum x1 -> x0, waiting for transfers between devices: 140 us -> none  [shards(): dec_total = lax.psum(dec_part, 'dp')]
    ppermute x0 -> x5, waiting for transfers between devices: none -> 71.1 us  [shards(): lax.ppermute(dec_total, 'dp', [(dev, dev ^ hop) for dev in range(32)])]
    all_to_all x1 -> x0, blocking collectives: 23.2 us -> none  [share_sum(): lax.all_to_all(blocks, axis, 0, 0).astype(jnp.float32)]
    ppermute x0 -> x5, starting transfers between devices: none -> 20.1 us  [shards(): lax.ppermute(dec_total, 'dp', [(dev, dev ^ hop) for dev in range(32)])]
    all_to_all x3, waiting for transfers between devices: 38.3 us -> 24.2 us  [spread(): lax.all_to_all(jnp.broadcast_to(block[None], (size,) + block.shape), axis...]
    all_to_all x0 -> x1, starting transfers between devices: none -> 8.36 us  [share_sum(): lax.all_to_all(blocks, axis, 0, 0).astype(jnp.float32)]
  transfers between devices with their start and end apart: 12 -> 17, of which waited for: 9 -> 11; matrix products, arithmetic and copies ran while one was open for 5% -> 7% of each run, Pallas kernels for 0% -> 0%
where the time goes in v1:
time: 298 us; the launch traced here: 297 us
  waiting for transfers between devices  135 us (45%)
  starting transfers between devices  74.7 us (25%)
  matrix products  26.7 us (9%)
  blocking collectives  22.3 us (7%)
  between operations  14 us (5%)
  other arithmetic  13.2 us (4%)
  local copies, waits for them, and re-layouts  10.8 us (4%)
    ppermute x5, waiting for transfers between devices, shards(): lax.ppermute(dec_total, 'dp', [(dev, dev ^ hop) for dev in range(32)])  71.1 us
    all_to_all x3, waiting for transfers between devices, spread(): lax.all_to_all(jnp.broadcast_to(block[None], (size,) + block.shape), axis...  24.2 us
    all_gather x1, waiting for transfers between devices, shards(): out_part = lax.all_gather(out_part, 'mp', axis=0, tiled=True)  23.1 us
    all_to_all x1, blocking collectives, spread(): lax.all_to_all(jnp.broadcast_to(block[None], (size,) + block.shape), axis...  22.3 us
    all_to_all x3, starting transfers between devices, spread(): lax.all_to_all(jnp.broadcast_to(block[None], (size,) + block.shape), axis...  20.7 us
    ppermute x5, starting transfers between devices, swap(): return lax.ppermute(block, 'segment', [(0, 1), (1, 0)])  20.6 us
    ppermute x5, starting transfers between devices, shards(): lax.ppermute(dec_total, 'dp', [(dev, dev ^ hop) for dev in range(32)])  20.1 us
    all_to_all x1, waiting for transfers between devices, shards(): lax.all_to_all(partial.reshape(mp, shard_rows, features), 'mp', 0, 0)  14.9 us
  transfers between devices with their start and end apart: 17, of which 11 were waited for; matrix products, arithmetic and copies ran while one was open for 7% of the time, Pallas kernels for 0%

profile of v1, /device:TPU:1, one launch (start us, length us, event | category | flops | bytes accessed | tf_op | source)
XLA Modules:
  0.0 296.8 jit_solution(8018879356043347106)
XLA Ops:
  8.5 10.9 %all-to-all-start = ((bf16[8,32,1280]{2,1,0:T(8,128)(2,1)}), bf16[8,32,1280]{2,1,0:T(8,128)(2,1)S(1)}, u32[]{:S(2)}, u32[]{:S(2)}) async-start(bf16[8,32,1280]{2,1,0:T(8,128)(2,1)} %broadcast_in_dim.31), calls=%async_computation | async-start | bytes 1310720 | tf_op jit(solution)/shard_map/all_to_all | solution.py:104
  19.4 2.9 collective-permute-start
  27.3 12.9 %all-to-all-done = bf16[8,32,1280]{2,1,0:T(8,128)(2,1)S(1)} async-done(((bf16[8,32,1280]{2,1,0:T(8,128)(2,1)}), bf16[8,32,1280]{2,1,0:T(8,128)(2,1)S(1)}, u32[]{:S(2)}, u32[]{:S(2)}) %all-to-all-start) | async-done | bytes 655392 | tf_op jit(solution)/shard_map/all_to_all | solution.py:104
  41.4 1.5 broadcast_select_fusion
  44.4 23.1 %all-gather.2.cloned.1.call-done = bf16[1024,640]{1,0:T(8,128)(2,1)} async-done(((bf16[128,640]{1,0:T(8,128)(2,1)}), bf16[1024,640]{1,0:T(8,128)(2,1)}) %all-gather.2.cloned.1.call-update) | async-done | bytes 1310736 | tf_op jit(solution)/shard_map/all_gather | solution.py:152
  67.5 7.2 %collective-permute-start.2 = (bf16[1024,640]{1,0:T(8,128)(2,1)}, bf16[1024,640]{1,0:T(8,128)(2,1)}, u32[]{:S(2)}, u32[]{:S(2)}) collective-permute-start(bf16[1024,640]{1,0:T(8,128)(2,1)} %all-gather.2.cloned.1.call-done), channel_id=1, source_target_pairs={{0,8},{8,0},{1,9},{9,1},{2,10},{10,2},{3,11},{11,3},{4,12},{12,4},... | collective-permute-start | bytes 3932168 | tf_op jit(solution)/shard_map/ppermute | solution.py:112
  77.3 3.9 %all-to-all-start.1 = ((bf16[8,256,128]{1,2,0:T(8,128)(2,1)}), bf16[8,256,128]{1,2,0:T(8,128)(2,1)S(1)}, u32[]{:S(2)}, u32[]{:S(2)}) async-start(bf16[8,256,128]{1,2,0:T(8,128)(2,1)} %broadcast_in_dim.34), calls=%async_computation.1 | async-start | bytes 1048576 | tf_op jit(solution)/shard_map/all_to_all | solution.py:104
  84.6 1.8 convolution_convert_fusion.11
  87.9 11.3 %all-to-all-done.1 = bf16[8,256,128]{1,2,0:T(8,128)(2,1)S(1)} async-done(((bf16[8,256,128]{1,2,0:T(8,128)(2,1)}), bf16[8,256,128]{1,2,0:T(8,128)(2,1)S(1)}, u32[]{:S(2)}, u32[]{:S(2)}) %all-to-all-start.1) | async-done | bytes 524320 | tf_op jit(solution)/shard_map/all_to_all | solution.py:104
  99.2 1.9 fusion.72
  101.1 1.9 broadcast_select_fusion.7
  106.2 2.4 fusion.25
  113.9 2.2 fusion.2
  116.1 3.5 %all-to-all-start.2 = ((bf16[8,32,1280]{2,1,0:T(8,128)(2,1)}), bf16[8,32,1280]{2,1,0:T(8,128)(2,1)S(1)}, u32[]{:S(2)}, u32[]{:S(2)}) async-start(bf16[8,32,1280]{2,1,0:T(8,128)(2,1)} %bitcast.37), calls=%async_computation.2 | async-start | bytes 1310720 | tf_op jit(solution)/shard_map/all_to_all | solution.py:210
  121.4 2.4 collective-permute-start.3
  125.4 14.9 %all-to-all-done.2 = bf16[8,32,1280]{2,1,0:T(8,128)(2,1)S(1)} async-done(((bf16[8,32,1280]{2,1,0:T(8,128)(2,1)}), bf16[8,32,1280]{2,1,0:T(8,128)(2,1)S(1)}, u32[]{:S(2)}, u32[]{:S(2)}) %all-to-all-start.2) | async-done | bytes 655392 | tf_op jit(solution)/shard_map/all_to_all | solution.py:210
  140.8 22.3 %all_to_all.30 = bf16[8,32,1280]{2,1,0:T(8,128)(2,1)S(1)} all-to-all(bf16[8,32,1280]{2,1,0:T(8,128)(2,1)S(1)} %broadcast_in_dim.37), channel_id=1, replica_groups=mesh['dp'=32,'segment'=2,'mp'=8] {'mp'}, dimensions={0} | all-to-all | bytes 1310720 | tf_op jit(solution)/shard_map/all_to_all | solution.py:104
  168.3 1.7 fusion.16
  170.5 3.2 %collective-permute-start.4 = (bf16[384,640]{1,0:T(8,128)(2,1)S(1)}, bf16[384,640]{1,0:T(8,128)(2,1)S(1)}, u32[]{:S(2)}, u32[]{:S(2)}) collective-permute-start(bf16[384,640]{1,0:T(8,128)(2,1)S(1)} %select_convert_fusion), channel_id=1, source_target_pairs={{0,8},{8,0},{1,9},{9,1},{2,10},{10,2},{3,11},{11,3},{4,12},{12,4},... | collective-permute-start | bytes 1474568 | tf_op jit(solution)/shard_map/ppermute | solution.py:112
  173.7 3.1 %collective-permute-start.5 = (bf16[384,640]{1,0:T(8,128)(2,1)S(1)}, bf16[384,640]{1,0:T(8,128)(2,1)S(1)}, u32[]{:S(2)}, u32[]{:S(2)}) collective-permute-start(bf16[384,640]{1,0:T(8,128)(2,1)S(1)} %add_convert_fusion.2), channel_id=1, source_target_pairs={{0,16},{16,0},{32,48},{48,32},{64,80},{80,64},{96,112},{112,96},{1... | collective-permute-start | bytes 1474568 | tf_op jit(solution)/shard_map/ppermute | solution.py:214
  177.9 8.4 %all-to-all-start.4 = ((bf16[32,8,8,128]{3,2,1,0:T(8,128)(2,1)}), bf16[32,8,8,128]{3,2,1,0:T(8,128)(2,1)S(1)}, u32[]{:S(2)}, u32[]{:S(2)}) async-start(bf16[32,8,8,128]{3,2,1,0:T(8,128)(2,1)} %bitcast.53), calls=%async_computation.4 | async-start | bytes 1048576 | tf_op jit(solution)/shard_map/all_to_all | solution.py:108
  186.2 2.2 collective-permute-done.5
  188.6 4.0 %collective-permute-start.6 = (bf16[384,640]{1,0:T(8,128)(2,1)S(1)}, bf16[384,640]{1,0:T(8,128)(2,1)S(1)}, u32[]{:S(2)}, u32[]{:S(2)}) collective-permute-start(bf16[384,640]{1,0:T(8,128)(2,1)S(1)} %add.150), channel_id=1, source_target_pairs={{0,32},{16,48},{32,0},{48,16},{64,96},{80,112},{96,64},{112,80},{1... | collective-permute-start | bytes 1474568 | tf_op jit(solution)/shard_map/ppermute | solution.py:214
  192.6 28.4 %collective-permute-done.6 = bf16[384,640]{1,0:T(8,128)(2,1)S(1)} collective-permute-done((bf16[384,640]{1,0:T(8,128)(2,1)S(1)}, bf16[384,640]{1,0:T(8,128)(2,1)S(1)}, u32[]{:S(2)}, u32[]{:S(2)}) %collective-permute-start.6) | collective-permute-done | bytes 491552 | tf_op jit(solution)/shard_map/ppermute | solution.py:214
  221.1 5.4 %collective-permute-start.7 = (bf16[384,640]{1,0:T(8,128)(2,1)S(1)}, bf16[384,640]{1,0:T(8,128)(2,1)S(1)}, u32[]{:S(2)}, u32[]{:S(2)}) collective-permute-start(bf16[384,640]{1,0:T(8,128)(2,1)S(1)} %add.151), channel_id=1, source_target_pairs={{0,64},{16,80},{32,96},{48,112},{64,0},{80,16},{96,32},{112,48},{1... | collective-permute-start | bytes 1474568 | tf_op jit(solution)/shard_map/ppermute | solution.py:214
  227.5 6.0 %all-to-all-start.5 = ((bf16[32,8,8,128]{3,2,1,0:T(8,128)(2,1)}), bf16[32,8,8,128]{3,2,1,0:T(8,128)(2,1)S(1)}, u32[]{:S(2)}, u32[]{:S(2)}) async-start(bf16[32,8,8,128]{3,2,1,0:T(8,128)(2,1)} %broadcast_in_dim.42), calls=%async_computation.5 | async-start | bytes 1048576 | tf_op jit(solution)/shard_map/all_to_all | solution.py:104
  233.5 19.7 %collective-permute-done.7 = bf16[384,640]{1,0:T(8,128)(2,1)S(1)} collective-permute-done((bf16[384,640]{1,0:T(8,128)(2,1)S(1)}, bf16[384,640]{1,0:T(8,128)(2,1)S(1)}, u32[]{:S(2)}, u32[]{:S(2)}) %collective-permute-start.7) | collective-permute-done | bytes 491552 | tf_op jit(solution)/shard_map/ppermute | solution.py:214
  253.4 3.1 %collective-permute-start.8 = (bf16[384,640]{1,0:T(8,128)(2,1)S(1)}, bf16[384,640]{1,0:T(8,128)(2,1)S(1)}, u32[]{:S(2)}, u32[]{:S(2)}) collective-permute-start(bf16[384,640]{1,0:T(8,128)(2,1)S(1)} %add.152), channel_id=1, source_target_pairs={{0,128},{16,144},{32,160},{48,176},{64,192},{80,208},{96,224},{112... | collective-permute-start | bytes 1474568 | tf_op jit(solution)/shard_map/ppermute | solution.py:214
  256.5 11.3 %collective-permute-done.8 = bf16[384,640]{1,0:T(8,128)(2,1)S(1)} collective-permute-done((bf16[384,640]{1,0:T(8,128)(2,1)S(1)}, bf16[384,640]{1,0:T(8,128)(2,1)S(1)}, u32[]{:S(2)}, u32[]{:S(2)}) %collective-permute-start.8) | collective-permute-done | bytes 491552 | tf_op jit(solution)/shard_map/ppermute | solution.py:214
  267.9 4.5 %collective-permute-start.9 = (bf16[384,640]{1,0:T(8,128)(2,1)S(1)}, bf16[384,640]{1,0:T(8,128)(2,1)S(1)}, u32[]{:S(2)}, u32[]{:S(2)}) collective-permute-start(bf16[384,640]{1,0:T(8,128)(2,1)S(1)} %add.153), channel_id=1, source_target_pairs={{0,256},{16,272},{32,288},{48,304},{64,320},{80,336},{96,352},{112... | collective-permute-start | bytes 1474568 | tf_op jit(solution)/shard_map/ppermute | solution.py:214
  272.5 9.5 %collective-permute-done.9 = bf16[384,640]{1,0:T(8,128)(2,1)S(1)} collective-permute-done((bf16[384,640]{1,0:T(8,128)(2,1)S(1)}, bf16[384,640]{1,0:T(8,128)(2,1)S(1)}, u32[]{:S(2)}, u32[]{:S(2)}) %collective-permute-start.9) | collective-permute-done | bytes 491552 | tf_op jit(solution)/shard_map/ppermute | solution.py:214
  282.0 4.9 %collective-permute-start.10 = (bf16[384,640]{1,0:T(8,128)(2,1)S(1)}, bf16[384,640]{1,0:T(8,128)(2,1)S(1)}, u32[]{:S(2)}, u32[]{:S(2)}) collective-permute-start(bf16[384,640]{1,0:T(8,128)(2,1)S(1)} %broadcast_select_fusion.4), channel_id=1, source_target_pairs={{0,8},{8,0},{1,9},{9,1},{2,10},{10,2},{3,11},{11,3},{4,12},{12,4},... | collective-permute-start | bytes 1474568 | tf_op jit(solution)/shard_map/ppermute | solution.py:112
  (142 shorter events, 40.4 us)
Async XLA Ops:
  6.5 75.9 %copy-start = (bf16[2,64,1280]{2,1,0:T(8,128)(2,1)S(1)}, bf16[2,64,1280]{2,1,0:T(8,128)(2,1)}, u32[]{:S(2)}) copy-start(bf16[2,64,1280]{2,1,0:T(8,128)(2,1)} %param.10) | copy-start | bytes 983044
  6.5 12.9 %copy-start.4 = (bf16[1,4,128,1280]{3,2,1,0:T(8,128)(2,1)S(1)}, bf16[1,4,128,1280]{3,2,1,0:T(8,128)(2,1)}, u32[]{:S(2)}) copy-start(bf16[1,4,128,1280]{3,2,1,0:T(8,128)(2,1)} %param.13) | copy-start | bytes 3932164
  6.5 17.1 %copy-start.15 = (s32[2,1,4]{2,1,0:T(1,128)S(1)}, s32[2,1,4]{2,1,0:T(1,128)}, u32[]{:S(2)}) copy-start(s32[2,1,4]{2,1,0:T(1,128)} %param.11) | copy-start | bytes 100
  6.5 17.1 %copy-start.16 = (s32[2,1,4]{2,1,0:T(1,128)S(1)}, s32[2,1,4]{2,1,0:T(1,128)}, u32[]{:S(2)}) copy-start(s32[2,1,4]{2,1,0:T(1,128)} %param.12) | copy-start | bytes 100
  6.5 17.4 %copy-start.7 = (bf16[2,64,1280]{2,1,0:T(8,128)(2,1)S(1)}, bf16[2,64,1280]{2,1,0:T(8,128)(2,1)}, u32[]{:S(2)}) copy-start(bf16[2,64,1280]{2,1,0:T(8,128)(2,1)} %param.9) | copy-start | bytes 983044
  7.6 18.3 %copy-start.12 = (f32[3,1280]{1,0:T(4,128)S(1)}, f32[3,1280]{1,0:T(4,128)}, u32[]{:S(2)}) copy-start(f32[3,1280]{1,0:T(4,128)} %param.15) | copy-start | bytes 46084
  7.6 18.3 %copy-start.13 = (f32[3,1280]{1,0:T(4,128)S(1)}, f32[3,1280]{1,0:T(4,128)}, u32[]{:S(2)}) copy-start(f32[3,1280]{1,0:T(4,128)} %param.14) | copy-start | bytes 46084
  8.5 31.6 %all-to-all-start = ((bf16[8,32,1280]{2,1,0:T(8,128)(2,1)}), bf16[8,32,1280]{2,1,0:T(8,128)(2,1)S(1)}, u32[]{:S(2)}, u32[]{:S(2)}) async-start(bf16[8,32,1280]{2,1,0:T(8,128)(2,1)} %broadcast_in_dim.31), calls=%async_computation | async-start | bytes 1310720 | tf_op jit(solution)/shard_map/all_to_all | solution.py:104
  19.3 48.2 %all-gather.2.cloned.1.call-start = ((), (), s32[]{:S(2)}) async-start(), calls=%async_computation.6 | async-start | bytes 1474560 | tf_op jit(solution)/shard_map/all_gather | solution.py:152
  19.4 21.6 %collective-permute-start = (bf16[4,128,1280]{2,1,0:T(8,128)(2,1)S(1)}, bf16[4,128,1280]{2,1,0:T(8,128)(2,1)}, u32[]{:S(2)}, u32[]{:S(2)}) collective-permute-start(bf16[4,128,1280]{2,1,0:T(8,128)(2,1)S(1)} %bitcast.176), channel_id=1, source_target_pairs={{0,8},{8,0},{1,9},{9,1},{2,10},{10,2},{3,11},{11,3},{4,12},{12,4},... | collective-permute-start | bytes 3932168 | tf_op jit(solution)/shard_map/ppermute | solution.py:112
  22.3 4.2 %collective-permute-start.1 = (bf16[128,640]{1,0:T(8,128)(2,1)S(1)}, bf16[128,640]{1,0:T(8,128)(2,1)S(1)}, u32[]{:S(2)}, u32[]{:S(2)}) collective-permute-start(bf16[128,640]{1,0:T(8,128)(2,1)S(1)} %slice_bitcast_fusion.18), channel_id=1, source_target_pairs={{0,8},{1,9},{2,10},{3,11},{4,12},{5,13},{6,14},{7,15},{16,24},{17,... | collective-permute-start | bytes 491528 | tf_op jit(solution)/shard_map/ppermute | solution.py:150
  24.0 1.8 copy-start.14
  25.3 50.6 %copy-start.8 = (pred[256,256]{0,1:T(8,128)(4,1)}, pred[256,256]{0,1:T(8,128)(4,1)S(1)}, u32[]{:S(2)}) copy-start(pred[256,256]{0,1:T(8,128)(4,1)S(1)} %broadcast_compare_fusion) | copy-start | bytes 196612
  42.9 41.7 %copy-start.2 = (bf16[4,128,1280]{2,1,0:T(8,128)(2,1)}, bf16[4,128,1280]{2,1,0:T(8,128)(2,1)S(1)}, u32[]{:S(2)}) copy-start(bf16[4,128,1280]{2,1,0:T(8,128)(2,1)S(1)} %get-tuple-element.21) | copy-start | bytes 3932164
  43.3 32.6 %copy-start.21 = (bf16[256,128]{0,1:T(8,128)(2,1)}, bf16[256,128]{0,1:T(8,128)(2,1)S(1)}, u32[]{:S(2)}) copy-start(bf16[256,128]{0,1:T(8,128)(2,1)S(1)} %convolution_convert_fusion.4) | copy-start | bytes 196612
  44.0 32.5 %copy-start.17 = (bf16[256,128]{0,1:T(8,128)(2,1)}, bf16[256,128]{0,1:T(8,128)(2,1)S(1)}, u32[]{:S(2)}) copy-start(bf16[256,128]{0,1:T(8,128)(2,1)S(1)} %convolution_convert_fusion.6) | copy-start | bytes 196612
  44.4 32.1 %copy-start.19 = (bf16[256,128]{0,1:T(8,128)(2,1)}, bf16[256,128]{0,1:T(8,128)(2,1)S(1)}, u32[]{:S(2)}) copy-start(bf16[256,128]{0,1:T(8,128)(2,1)S(1)} %convolution_convert_fusion.5) | copy-start | bytes 196612
  67.5 31.7 %collective-permute-start.2 = (bf16[1024,640]{1,0:T(8,128)(2,1)}, bf16[1024,640]{1,0:T(8,128)(2,1)}, u32[]{:S(2)}, u32[]{:S(2)}) collective-permute-start(bf16[1024,640]{1,0:T(8,128)(2,1)} %all-gather.2.cloned.1.call-done), channel_id=1, source_target_pairs={{0,8},{8,0},{1,9},{9,1},{2,10},{10,2},{3,11},{11,3},{4,12},{12,4},... | collective-permute-start | bytes 3932168 | tf_op jit(solution)/shard_map/ppermute | solution.py:112
  77.3 21.9 %all-to-all-start.1 = ((bf16[8,256,128]{1,2,0:T(8,128)(2,1)}), bf16[8,256,128]{1,2,0:T(8,128)(2,1)S(1)}, u32[]{:S(2)}, u32[]{:S(2)}) async-start(bf16[8,256,128]{1,2,0:T(8,128)(2,1)} %broadcast_in_dim.34), calls=%async_computation.1 | async-start | bytes 1048576 | tf_op jit(solution)/shard_map/all_to_all | solution.py:104
  104.0 1.8 copy-start.9
  116.1 24.2 %all-to-all-start.2 = ((bf16[8,32,1280]{2,1,0:T(8,128)(2,1)}), bf16[8,32,1280]{2,1,0:T(8,128)(2,1)S(1)}, u32[]{:S(2)}, u32[]{:S(2)}) async-start(bf16[8,32,1280]{2,1,0:T(8,128)(2,1)} %bitcast.37), calls=%async_computation.2 | async-start | bytes 1310720 | tf_op jit(solution)/shard_map/all_to_all | solution.py:210
  121.4 3.8 %collective-permute-start.3 = (bf16[384,640]{1,0:T(8,128)(2,1)S(1)}, bf16[384,640]{1,0:T(8,128)(2,1)S(1)}, u32[]{:S(2)}, u32[]{:S(2)}) collective-permute-start(bf16[384,640]{1,0:T(8,128)(2,1)S(1)} %select_convert_fusion.1), channel_id=1, source_target_pairs={{0,8},{8,0},{1,9},{9,1},{2,10},{10,2},{3,11},{11,3},{4,12},{12,4},... | collective-permute-start | bytes 1474568 | tf_op jit(solution)/shard_map/ppermute | solution.py:112
  164.7 1.7 copy-start.22
  170.5 6.4 %collective-permute-start.4 = (bf16[384,640]{1,0:T(8,128)(2,1)S(1)}, bf16[384,640]{1,0:T(8,128)(2,1)S(1)}, u32[]{:S(2)}, u32[]{:S(2)}) collective-permute-start(bf16[384,640]{1,0:T(8,128)(2,1)S(1)} %select_convert_fusion), channel_id=1, source_target_pairs={{0,8},{8,0},{1,9},{9,1},{2,10},{10,2},{3,11},{11,3},{4,12},{12,4},... | collective-permute-start | bytes 1474568 | tf_op jit(solution)/shard_map/ppermute | solution.py:112
  173.7 14.7 %collective-permute-start.5 = (bf16[384,640]{1,0:T(8,128)(2,1)S(1)}, bf16[384,640]{1,0:T(8,128)(2,1)S(1)}, u32[]{:S(2)}, u32[]{:S(2)}) collective-permute-start(bf16[384,640]{1,0:T(8,128)(2,1)S(1)} %add_convert_fusion.2), channel_id=1, source_target_pairs={{0,16},{16,0},{32,48},{48,32},{64,80},{80,64},{96,112},{112,96},{1... | collective-permute-start | bytes 1474568 | tf_op jit(solution)/shard_map/ppermute | solution.py:214
  177.9 48.6 %all-to-all-start.4 = ((bf16[32,8,8,128]{3,2,1,0:T(8,128)(2,1)}), bf16[32,8,8,128]{3,2,1,0:T(8,128)(2,1)S(1)}, u32[]{:S(2)}, u32[]{:S(2)}) async-start(bf16[32,8,8,128]{3,2,1,0:T(8,128)(2,1)} %bitcast.53), calls=%async_computation.4 | async-start | bytes 1048576 | tf_op jit(solution)/shard_map/all_to_all | solution.py:108
  188.6 32.4 %collective-permute-start.6 = (bf16[384,640]{1,0:T(8,128)(2,1)S(1)}, bf16[384,640]{1,0:T(8,128)(2,1)S(1)}, u32[]{:S(2)}, u32[]{:S(2)}) collective-permute-start(bf16[384,640]{1,0:T(8,128)(2,1)S(1)} %add.150), channel_id=1, source_target_pairs={{0,32},{16,48},{32,0},{48,16},{64,96},{80,112},{96,64},{112,80},{1... | collective-permute-start | bytes 1474568 | tf_op jit(solution)/shard_map/ppermute | solution.py:214
  221.1 32.1 %collective-permute-start.7 = (bf16[384,640]{1,0:T(8,128)(2,1)S(1)}, bf16[384,640]{1,0:T(8,128)(2,1)S(1)}, u32[]{:S(2)}, u32[]{:S(2)}) collective-permute-start(bf16[384,640]{1,0:T(8,128)(2,1)S(1)} %add.151), channel_id=1, source_target_pairs={{0,64},{16,80},{32,96},{48,112},{64,0},{80,16},{96,32},{112,48},{1... | collective-permute-start | bytes 1474568 | tf_op jit(solution)/shard_map/ppermute | solution.py:214
  227.5 44.9 %all-to-all-start.5 = ((bf16[32,8,8,128]{3,2,1,0:T(8,128)(2,1)}), bf16[32,8,8,128]{3,2,1,0:T(8,128)(2,1)S(1)}, u32[]{:S(2)}, u32[]{:S(2)}) async-start(bf16[32,8,8,128]{3,2,1,0:T(8,128)(2,1)} %broadcast_in_dim.42), calls=%async_computation.5 | async-start | bytes 1048576 | tf_op jit(solution)/shard_map/all_to_all | solution.py:104
  253.4 14.4 %collective-permute-start.8 = (bf16[384,640]{1,0:T(8,128)(2,1)S(1)}, bf16[384,640]{1,0:T(8,128)(2,1)S(1)}, u32[]{:S(2)}, u32[]{:S(2)}) collective-permute-start(bf16[384,640]{1,0:T(8,128)(2,1)S(1)} %add.152), channel_id=1, source_target_pairs={{0,128},{16,144},{32,160},{48,176},{64,192},{80,208},{96,224},{112... | collective-permute-start | bytes 1474568 | tf_op jit(solution)/shard_map/ppermute | solution.py:214
  267.9 14.0 %collective-permute-start.9 = (bf16[384,640]{1,0:T(8,128)(2,1)S(1)}, bf16[384,640]{1,0:T(8,128)(2,1)S(1)}, u32[]{:S(2)}, u32[]{:S(2)}) collective-permute-start(bf16[384,640]{1,0:T(8,128)(2,1)S(1)} %add.153), channel_id=1, source_target_pairs={{0,256},{16,272},{32,288},{48,304},{64,320},{80,336},{96,352},{112... | collective-permute-start | bytes 1474568 | tf_op jit(solution)/shard_map/ppermute | solution.py:214
  282.0 6.4 %collective-permute-start.10 = (bf16[384,640]{1,0:T(8,128)(2,1)S(1)}, bf16[384,640]{1,0:T(8,128)(2,1)S(1)}, u32[]{:S(2)}, u32[]{:S(2)}) collective-permute-start(bf16[384,640]{1,0:T(8,128)(2,1)S(1)} %broadcast_select_fusion.4), channel_id=1, source_target_pairs={{0,8},{8,0},{1,9},{9,1},{2,10},{10,2},{3,11},{11,3},{4,12},{12,4},... | collective-permute-start | bytes 1474568 | tf_op jit(solution)/shard_map/ppermute | solution.py:112
  (11 other events, 15.3 us)
Sparse Core Ops, SparseCore 0:
  27.4 40.0 all-gather.1
